TPU v7x, 512 devices: a whole 4x4x16 slice. The times are simulated.
512 devices in a mesh: blk: 64 (over z, x_lo, core), rep: 8 (over y, x_hi).
Axes of the slice: x: 4 (x_hi: 2, x_lo: 2; x = x_hi * 2 + x_lo), y: 4, z: 16, core: 2. Of those that a mesh axis runs over, the one named last changes fastest.
Arguments:
- features: bfloat16 [65536, 256], P(('blk', 'rep')), may hold values from -6 to 6
- out_grad: bfloat16 [65536, 256], P('blk'), may hold values from -4 to 4
- weight: bfloat16 [256, 256], replicated, may hold values from -0.375 to 0.375
- block_words: int32 [64, 64, 8, 16, 128], P('blk', 'rep'), may hold values from 0 to 255
- block_coords: int32 [64, 64, 2, 8], P('blk', 'rep'), may hold values from 0 to 7, as said below
- block_counts: int32 [64, 64], P('blk', 'rep'), may hold values from 1 to 8, as said below
- degrees: int32 [65536], P('blk'), may hold values from 1 to 127
Outputs:
- input_grad: bfloat16 [65536, 256], P(('blk', 'rep'))
- weight_grad: float32 [256, 256], replicated
Inputs may be any that keep to these rules, and one draw needn't show every extreme that they name: `block_coords`: within one slab pair the 8 slots name distinct pairs of row block and column block. `block_counts`: the 8 slab pairs of one device include one in which all 8 slots are live.
All inputs are finite; a program needn't handle non-finite values.
Results may differ from a plain program's by a relative error of at most 0.015.
Values may be sent and summed in bfloat16 or wider, within the bound.
A program may use at most 64 MiB of HBM per device.

v0:
```python
import math
import jax
import jax.numpy as jnp
from jax import lax
from jax.sharding import PartitionSpec as P


def from_behind(block, axis, distance):
    devices = range(lax.axis_size(axis))
    route = [((i - distance) % len(devices), i) for i in devices]
    return lax.ppermute(block, axis, route)


def unpack_block(slot_words):
    shifts = jnp.arange(8, dtype=jnp.int32)
    bit_values = jnp.bitwise_and(
        jnp.right_shift(slot_words[:, :, None, :], shifts[None, None, :, None]), 1
    )
    return bit_values.reshape(slot_words.shape[0], 128, 128).astype(jnp.bfloat16)


def per_device(features, out_grad, weight, block_words, block_coords, block_counts, degrees):
    slab_rows, width = out_grad.shape
    row_blocks = slab_rows // 128
    group_size = lax.axis_size("rep")
    step_count = lax.axis_size("blk") // group_size
    rep_index = lax.axis_index("rep")
    inverse_root = lax.rsqrt(degrees.astype(jnp.float32))
    scaled = (out_grad.astype(jnp.float32) * inverse_root[:, None]).astype(jnp.bfloat16)
    column_ids = jnp.arange(row_blocks, dtype=jnp.int32)
    slot_total = block_words.shape[2]
    slot_ids = jnp.arange(slot_total, dtype=jnp.int32)

    def add_slot(accumulated, source_slab, slot_index):
        slot_words = lax.dynamic_index_in_dim(block_words[0], slot_index, 0, keepdims=False)
        coords = lax.dynamic_index_in_dim(block_coords[0], slot_index, 0, keepdims=False)
        live_count = lax.dynamic_index_in_dim(block_counts[0], slot_index, 0, keepdims=False)
        picked = jnp.take(source_slab.reshape(row_blocks, 128, width), coords[0], axis=0)
        transposed = unpack_block(slot_words)
        contrib = jnp.einsum("bvu,buf->bvf", transposed, picked, preferred_element_type=jnp.float32)
        live_slots = slot_ids < live_count
        placement = ((coords[1][:, None] == column_ids[None, :]) & live_slots[:, None]).astype(
            jnp.float32
        )
        return accumulated + jnp.einsum("bc,bvf->cvf", placement, contrib)

    empty = jnp.zeros((row_blocks, 128, width), jnp.float32)
    current = scaled
    for bit in range(group_size.bit_length() - 1):
        shifted = from_behind(current, "blk", -(1 << bit) * step_count)
        current = jnp.where(
            jnp.bitwise_and(jnp.right_shift(rep_index, bit), 1) == 1, shifted, current
        )
    accumulated = add_slot(empty, current, 0)

    def advance(step_index, state_tuple):
        current, accumulated = state_tuple
        current = from_behind(current, "blk", -1)
        return (current, add_slot(accumulated, current, step_index))

    current, accumulated = lax.fori_loop(1, step_count, advance, (current, accumulated))
    partial_sums = accumulated.reshape(slab_rows, width)
    share_rows = slab_rows // group_size
    share_root = lax.dynamic_slice_in_dim(inverse_root, rep_index * share_rows, share_rows, 0)
    whole_sums = lax.psum(partial_sums, "rep")
    own_sums = lax.dynamic_slice_in_dim(whole_sums, rep_index * share_rows, share_rows, 0)
    aggregated = (own_sums * share_root[:, None]).astype(jnp.bfloat16)
    input_grad = lax.dot_general(
        aggregated, weight, (((1,), (1,)), ((), ())), preferred_element_type=jnp.float32
    ).astype(jnp.bfloat16)
    weight_term = lax.dot_general(
        features, aggregated, (((0,), (0,)), ((), ())), preferred_element_type=jnp.float32
    )
    node_total = slab_rows * lax.axis_size("blk")
    weight_grad = lax.psum(weight_term, ("blk", "rep")) * (1.0 / math.sqrt(node_total))
    return (input_grad, weight_grad)


def solution(mesh):
    return jax.shard_map(
        per_device,
        mesh=mesh,
        in_specs=(
            P(("blk", "rep"), None),
            P("blk", None),
            P(),
            P("blk", "rep", None, None, None),
            P("blk", "rep", None, None),
            P("blk", "rep"),
            P("blk"),
        ),
        out_specs=(P(("blk", "rep"), None), P()),
        check_vma=False,
    )
```

profile of v0, /device:TPU:4, one launch (start us, length us, event | category | flops | bytes accessed | tf_op | source)
XLA Modules:
  0.0 821.2 jit_solution(11861567313591803345)
XLA Ops:
  7.2 0.7 convert_rsqrt_fusion
  7.9 1.3 multiply_convert_fusion
  9.3 11.8 %collective-permute-start.1 = (bf16[1024,256]{1,0:T(8,128)(2,1)S(1)}, bf16[1024,256]{1,0:T(8,128)(2,1)S(1)}, u32[]{:S(2)}, u32[]{:S(2)}) collective-permute-start(bf16[1024,256]{1,0:T(8,128)(2,1)S(1)} %multiply_convert_fusion), channel_id=1, source_target_pairs={{64,0},{72,8},{80,16},{88,24},{96,32},{104,40},{112,48},{120,56},{... | collective-permute-start | bytes 1572872 | tf_op jit(solution)/shard_map/ppermute | solution.py:11
  21.1 22.4 %collective-permute-done.1 = bf16[1024,256]{1,0:T(8,128)(2,1)S(1)} collective-permute-done((bf16[1024,256]{1,0:T(8,128)(2,1)S(1)}, bf16[1024,256]{1,0:T(8,128)(2,1)S(1)}, u32[]{:S(2)}, u32[]{:S(2)}) %collective-permute-start.1) | collective-permute-done | bytes 524320 | tf_op jit(solution)/shard_map/ppermute | solution.py:11
  43.8 6.3 collective-permute-start.2
  50.3 0.7 compare_and_fusion.1
  51.0 40.0 %collective-permute-done.2 = bf16[1024,256]{1,0:T(8,128)(2,1)S(1)} collective-permute-done((bf16[1024,256]{1,0:T(8,128)(2,1)S(1)}, bf16[1024,256]{1,0:T(8,128)(2,1)S(1)}, u32[]{:S(2)}, u32[]{:S(2)}) %collective-permute-start.2) | collective-permute-done | bytes 524320 | tf_op jit(solution)/shard_map/ppermute | solution.py:11
  91.1 5.0 collective-permute-start.3
  96.1 0.6 copy-done.3
  96.7 0.7 slice_bitcast_fusion.2
  97.4 0.8 slice_bitcast_fusion.1
  98.3 28.4 %collective-permute-done.3 = bf16[1024,256]{1,0:T(8,128)(2,1)S(1)} collective-permute-done((bf16[1024,256]{1,0:T(8,128)(2,1)S(1)}, bf16[1024,256]{1,0:T(8,128)(2,1)S(1)}, u32[]{:S(2)}, u32[]{:S(2)}) %collective-permute-start.3) | collective-permute-done | bytes 524320 | tf_op jit(solution)/shard_map/ppermute | solution.py:11
  126.8 0.6 gather_fusion.1
  128.1 121.5 %while.20 = (s32[]{:T(128)}, bf16[1024,256]{1,0:T(8,128)(2,1)S(1)}, f32[8,128,256]{2,0,1:T(8,128)S(1)}, s32[1,8,2,8]{3,2,1,0:T(2,128)}, s32[1,8]{1,0:T(1,128)S(1...) while((s32[]{:T(128)}, bf16[1024,256]{1,0:T(8,128)(2,1)S(1)}, ...), condition=%wide.region_1.3_spmd.clone.clone, body=%wide.region_0.2_spmd.clone.clone.sunk | while | flops 72221880 | bytes 8067647 | solution.py:61
  128.2 29.0 %collective-permute-start = (bf16[1024,256]{1,0:T(8,128)(2,1)S(1)}, bf16[1024,256]{1,0:T(8,128)(2,1)S(1)}, u32[]{:S(2)}, u32[]{:S(2)}) collective-permute-start(bf16[1024,256]{1,0:T(8,128)(2,1)S(1)} %get-tuple-element.308), channel_id=1, source_target_pairs={{8,0},{16,8},{24,16},{32,24},{40,32},{48,40},{56,48},{64,56},{72,6... | collective-permute-start | bytes 1572872 | tf_op jit(solution)/shard_map/while/body/eval_jaxpr/ppermute | solution.py:11
  157.2 0.6 constant_dynamic-slice_fusion.5
  157.8 0.7 constant_dynamic-slice_fusion.4
  158.6 0.7 iota_compare_fusion.5
  159.2 0.9 dynamic-slice_bitcast_fusion.2
  160.1 3.8 collective-permute-done
  163.9 0.6 gather_fusion
  165.3 5.9 collective-permute-start
  171.3 0.6 constant_dynamic-slice_fusion.5
  171.8 0.7 constant_dynamic-slice_fusion.4
  172.6 0.7 iota_compare_fusion.5
  173.3 0.9 dynamic-slice_bitcast_fusion.2
  174.2 3.8 collective-permute-done
  179.4 5.9 collective-permute-start
  185.3 0.6 constant_dynamic-slice_fusion.5
  185.9 0.7 constant_dynamic-slice_fusion.4
  186.7 0.7 iota_compare_fusion.5
  187.4 0.9 dynamic-slice_bitcast_fusion.2
  188.2 3.8 collective-permute-done
  193.4 5.9 collective-permute-start
  199.4 0.6 constant_dynamic-slice_fusion.5
  200.0 0.7 constant_dynamic-slice_fusion.4
  200.8 0.7 iota_compare_fusion.5
  201.4 0.9 dynamic-slice_bitcast_fusion.2
  202.3 3.8 collective-permute-done
  207.5 5.9 collective-permute-start
  213.4 0.6 constant_dynamic-slice_fusion.5
  214.0 0.7 constant_dynamic-slice_fusion.4
  214.8 0.7 iota_compare_fusion.5
  215.5 0.9 dynamic-slice_bitcast_fusion.2
  216.3 3.8 collective-permute-done
  221.6 5.9 collective-permute-start
  227.5 0.6 constant_dynamic-slice_fusion.5
  228.1 0.7 constant_dynamic-slice_fusion.4
  228.9 0.7 iota_compare_fusion.5
  229.6 0.9 dynamic-slice_bitcast_fusion.2
  230.4 3.8 collective-permute-done
  235.6 5.9 collective-permute-start
  241.6 0.6 constant_dynamic-slice_fusion.5
  242.2 0.7 constant_dynamic-slice_fusion.4
  242.9 0.7 iota_compare_fusion.5
  243.6 0.9 dynamic-slice_bitcast_fusion.2
  244.5 3.8 collective-permute-done
  249.7 1.3 copy.10
  251.2 97.1 %all-reduce.3.cloned.1.call-done = f32[1024,256]{1,0:T(8,128)} async-done(((f32[1024,256]{1,0:T(8,128)}), f32[1024,256]{1,0:T(8,128)}) %all-reduce.3.cloned.1.call-update) | async-done | bytes 1048592 | tf_op jit(solution)/shard_map/psum | solution.py:65
  348.3 1.9 convolution_bitcast_fusion
  350.2 1.8 convolution_convert_fusion
  352.0 460.6 %all-reduce.5.cloned.1.call-done = f32[256,256]{0,1:T(8,128)} async-done(((f32[256,256]{0,1:T(8,128)}), f32[256,256]{0,1:T(8,128)}) %all-reduce.5.cloned.1.call-update) | async-done | bytes 262160 | tf_op jit(solution)/shard_map/psum | solution.py:75
  812.6 1.0 broadcast_multiply_fusion
  813.6 0.8 copy.11
  (83 shorter events, 11.6 us)
Async XLA Ops:
  7.2 343.1 %copy-start = (bf16[256,256]{1,0:T(8,128)(2,1)S(1)}, bf16[256,256]{1,0:T(8,128)(2,1)}, u32[]{:S(2)}) copy-start(bf16[256,256]{1,0:T(8,128)(2,1)} %param.13) | copy-start | bytes 393220
  7.2 341.1 %all-reduce.3.cloned.1.call-start = ((), (), s32[]{:S(2)}) async-start(), calls=%async_computation | async-start | bytes 2097152 | tf_op jit(solution)/shard_map/psum | solution.py:65
  7.9 35.6 %copy-start.1 = (bf16[1024,256]{1,0:T(8,128)(2,1)S(1)}, bf16[1024,256]{1,0:T(8,128)(2,1)}, u32[]{:S(2)}) copy-start(bf16[1024,256]{1,0:T(8,128)(2,1)} %param.12) | copy-start | bytes 1572868
  9.3 34.2 %collective-permute-start.1 = (bf16[1024,256]{1,0:T(8,128)(2,1)S(1)}, bf16[1024,256]{1,0:T(8,128)(2,1)S(1)}, u32[]{:S(2)}, u32[]{:S(2)}) collective-permute-start(bf16[1024,256]{1,0:T(8,128)(2,1)S(1)} %multiply_convert_fusion), channel_id=1, source_target_pairs={{64,0},{72,8},{80,16},{88,24},{96,32},{104,40},{112,48},{120,56},{... | collective-permute-start | bytes 1572872 | tf_op jit(solution)/shard_map/ppermute | solution.py:11
  43.8 47.2 %collective-permute-start.2 = (bf16[1024,256]{1,0:T(8,128)(2,1)S(1)}, bf16[1024,256]{1,0:T(8,128)(2,1)S(1)}, u32[]{:S(2)}, u32[]{:S(2)}) collective-permute-start(bf16[1024,256]{1,0:T(8,128)(2,1)S(1)} %broadcast_select_fusion), channel_id=1, source_target_pairs={{128,0},{136,8},{144,16},{152,24},{160,32},{168,40},{176,48},{184,... | collective-permute-start | bytes 1572872 | tf_op jit(solution)/shard_map/ppermute | solution.py:11
  91.1 35.7 %collective-permute-start.3 = (bf16[1024,256]{1,0:T(8,128)(2,1)S(1)}, bf16[1024,256]{1,0:T(8,128)(2,1)S(1)}, u32[]{:S(2)}, u32[]{:S(2)}) collective-permute-start(bf16[1024,256]{1,0:T(8,128)(2,1)S(1)} %broadcast_select_fusion.1), channel_id=1, source_target_pairs={{256,0},{264,8},{272,16},{280,24},{288,32},{296,40},{304,48},{312,... | collective-permute-start | bytes 1572872 | tf_op jit(solution)/shard_map/ppermute | solution.py:11
  96.0 0.7 copy-start.3
  128.2 35.7 %collective-permute-start = (bf16[1024,256]{1,0:T(8,128)(2,1)S(1)}, bf16[1024,256]{1,0:T(8,128)(2,1)S(1)}, u32[]{:S(2)}, u32[]{:S(2)}) collective-permute-start(bf16[1024,256]{1,0:T(8,128)(2,1)S(1)} %get-tuple-element.308), channel_id=1, source_target_pairs={{8,0},{16,8},{24,16},{32,24},{40,32},{48,40},{56,48},{64,56},{72,6... | collective-permute-start | bytes 1572872 | tf_op jit(solution)/shard_map/while/body/eval_jaxpr/ppermute | solution.py:11
  165.3 12.6 %collective-permute-start = (bf16[1024,256]{1,0:T(8,128)(2,1)S(1)}, bf16[1024,256]{1,0:T(8,128)(2,1)S(1)}, u32[]{:S(2)}, u32[]{:S(2)}) collective-permute-start(bf16[1024,256]{1,0:T(8,128)(2,1)S(1)} %get-tuple-element.308), channel_id=1, source_target_pairs={{8,0},{16,8},{24,16},{32,24},{40,32},{48,40},{56,48},{64,56},{72,6... | collective-permute-start | bytes 1572872 | tf_op jit(solution)/shard_map/while/body/eval_jaxpr/ppermute | solution.py:11
  179.4 12.6 %collective-permute-start = (bf16[1024,256]{1,0:T(8,128)(2,1)S(1)}, bf16[1024,256]{1,0:T(8,128)(2,1)S(1)}, u32[]{:S(2)}, u32[]{:S(2)}) collective-permute-start(bf16[1024,256]{1,0:T(8,128)(2,1)S(1)} %get-tuple-element.308), channel_id=1, source_target_pairs={{8,0},{16,8},{24,16},{32,24},{40,32},{48,40},{56,48},{64,56},{72,6... | collective-permute-start | bytes 1572872 | tf_op jit(solution)/shard_map/while/body/eval_jaxpr/ppermute | solution.py:11
  193.4 12.6 %collective-permute-start = (bf16[1024,256]{1,0:T(8,128)(2,1)S(1)}, bf16[1024,256]{1,0:T(8,128)(2,1)S(1)}, u32[]{:S(2)}, u32[]{:S(2)}) collective-permute-start(bf16[1024,256]{1,0:T(8,128)(2,1)S(1)} %get-tuple-element.308), channel_id=1, source_target_pairs={{8,0},{16,8},{24,16},{32,24},{40,32},{48,40},{56,48},{64,56},{72,6... | collective-permute-start | bytes 1572872 | tf_op jit(solution)/shard_map/while/body/eval_jaxpr/ppermute | solution.py:11
  207.5 12.6 %collective-permute-start = (bf16[1024,256]{1,0:T(8,128)(2,1)S(1)}, bf16[1024,256]{1,0:T(8,128)(2,1)S(1)}, u32[]{:S(2)}, u32[]{:S(2)}) collective-permute-start(bf16[1024,256]{1,0:T(8,128)(2,1)S(1)} %get-tuple-element.308), channel_id=1, source_target_pairs={{8,0},{16,8},{24,16},{32,24},{40,32},{48,40},{56,48},{64,56},{72,6... | collective-permute-start | bytes 1572872 | tf_op jit(solution)/shard_map/while/body/eval_jaxpr/ppermute | solution.py:11
  221.6 12.6 %collective-permute-start = (bf16[1024,256]{1,0:T(8,128)(2,1)S(1)}, bf16[1024,256]{1,0:T(8,128)(2,1)S(1)}, u32[]{:S(2)}, u32[]{:S(2)}) collective-permute-start(bf16[1024,256]{1,0:T(8,128)(2,1)S(1)} %get-tuple-element.308), channel_id=1, source_target_pairs={{8,0},{16,8},{24,16},{32,24},{40,32},{48,40},{56,48},{64,56},{72,6... | collective-permute-start | bytes 1572872 | tf_op jit(solution)/shard_map/while/body/eval_jaxpr/ppermute | solution.py:11
  235.6 12.6 %collective-permute-start = (bf16[1024,256]{1,0:T(8,128)(2,1)S(1)}, bf16[1024,256]{1,0:T(8,128)(2,1)S(1)}, u32[]{:S(2)}, u32[]{:S(2)}) collective-permute-start(bf16[1024,256]{1,0:T(8,128)(2,1)S(1)} %get-tuple-element.308), channel_id=1, source_target_pairs={{8,0},{16,8},{24,16},{32,24},{40,32},{48,40},{56,48},{64,56},{72,6... | collective-permute-start | bytes 1572872 | tf_op jit(solution)/shard_map/while/body/eval_jaxpr/ppermute | solution.py:11
  251.0 97.3 %copy-start.2 = (bf16[128,256]{1,0:T(8,128)(2,1)S(1)}, bf16[128,256]{1,0:T(8,128)(2,1)}, u32[]{:S(2)}) copy-start(bf16[128,256]{1,0:T(8,128)(2,1)} %param.11) | copy-start | bytes 196612
  251.0 561.5 %all-reduce.5.cloned.1.call-start = ((), (), s32[]{:S(2)}) async-start(), calls=%async_computation.1 | async-start | bytes 524288 | tf_op jit(solution)/shard_map/psum | solution.py:75
Sparse Core Ops, SparseCore 0:
  251.2 97.1 all-reduce.2
  354.3 458.2 all-reduce.4
where the time goes:
time: 822 us; the launch traced here: 821 us
  waiting for transfers between devices  675 us (82%)
  starting transfers between devices  87.8 us (11%)
  local copies, waits for them, and re-layouts  24.9 us (3%)
  between operations  14.2 us (2%)
  matrix products  9.97 us (1%)
  other arithmetic  8.83 us (1%)
    psum x1, waiting for transfers between devices, per_device(): lax.psum(weight_term, ('blk', 'rep')) * (1.0 / math.sqrt(node_total))  461 us
    ppermute x10, waiting for transfers between devices, from_behind(): return lax.ppermute(block, axis, route)  117 us
    psum x1, waiting for transfers between devices, per_device(): whole_sums = lax.psum(partial_sums, 'rep')  97.1 us
    ppermute x10, starting transfers between devices, from_behind(): return lax.ppermute(block, axis, route)  87.7 us
  transfers between devices with their start and end apart: 12, of which 12 were waited for; matrix products, arithmetic and copies ran while one was open for 3% of the time, Pallas kernels for 0%

commit v1 on v0

--- a/solution.py
+++ b/solution.py
@@ -62,7 +62,7 @@
     partial_sums = accumulated.reshape(slab_rows, width)
     share_rows = slab_rows // group_size
     share_root = lax.dynamic_slice_in_dim(inverse_root, rep_index * share_rows, share_rows, 0)
-    whole_sums = lax.psum(partial_sums, "rep")
+    whole_sums = jnp.sum(lax.all_gather(partial_sums, "rep"), axis=0)
     own_sums = lax.dynamic_slice_in_dim(whole_sums, rep_index * share_rows, share_rows, 0)
     aggregated = (own_sums * share_root[:, None]).astype(jnp.bfloat16)
     input_grad = lax.dot_general(

time: 822 us -> 838 us (1.019)
  waiting for transfers between devices: 675 us -> 717 us
  starting transfers between devices: 87.8 us -> 58 us
    all_gather x0 -> x1, waiting for transfers between devices: none -> 114 us  [per_device(): whole_sums = jnp.sum(lax.all_gather(partial_sums, 'rep'), axis=0)]
    psum x1 -> x0, waiting for transfers between devices: 97.1 us -> none  [per_device(): whole_sums = lax.psum(partial_sums, 'rep')]
    ppermute x10, starting transfers between devices: 87.7 us -> 58 us  [from_behind(): return lax.ppermute(block, axis, route)]
    ppermute x10, waiting for transfers between devices: 117 us -> 146 us  [from_behind(): return lax.ppermute(block, axis, route)]
where the time goes in v1:
time: 838 us; the launch traced here: 836 us
  waiting for transfers between devices  717 us (86%)
  starting transfers between devices  58 us (7%)
  local copies, waits for them, and re-layouts  24.3 us (3%)
  other arithmetic  14.4 us (2%)
  between operations  14.2 us (2%)
    psum x1, waiting for transfers between devices, per_device(): lax.psum(weight_term, ('blk', 'rep')) * (1.0 / math.sqrt(node_total))  457 us
    ppermute x10, waiting for transfers between devices, from_behind(): return lax.ppermute(block, axis, route)  146 us
    all_gather x1, waiting for transfers between devices, per_device(): whole_sums = jnp.sum(lax.all_gather(partial_sums, 'rep'), axis=0)  114 us
    ppermute x10, starting transfers between devices, from_behind(): return lax.ppermute(block, axis, route)  58 us
  transfers between devices with their start and end apart: 12, of which 12 were waited for; matrix products, arithmetic and copies ran while one was open for 3% of the time, Pallas kernels for 0%

profile of v1, /device:TPU:4, one launch (start us, length us, event | category | flops | bytes accessed | tf_op | source)
XLA Modules:
  0.0 836.5 jit_solution(6066579211144297636)
XLA Ops:
  7.2 0.7 convert_rsqrt_fusion
  7.9 1.2 multiply_convert_fusion
  9.2 11.8 %collective-permute-start.1 = (bf16[1024,256]{1,0:T(8,128)(2,1)S(1)}, bf16[1024,256]{1,0:T(8,128)(2,1)S(1)}, u32[]{:S(2)}, u32[]{:S(2)}) collective-permute-start(bf16[1024,256]{1,0:T(8,128)(2,1)S(1)} %multiply_convert_fusion), channel_id=1, source_target_pairs={{64,0},{72,8},{80,16},{88,24},{96,32},{104,40},{112,48},{120,56},{... | collective-permute-start | bytes 1572872 | tf_op jit(solution)/shard_map/ppermute | solution.py:11
  21.0 22.4 %collective-permute-done.1 = bf16[1024,256]{1,0:T(8,128)(2,1)S(1)} collective-permute-done((bf16[1024,256]{1,0:T(8,128)(2,1)S(1)}, bf16[1024,256]{1,0:T(8,128)(2,1)S(1)}, u32[]{:S(2)}, u32[]{:S(2)}) %collective-permute-start.1) | collective-permute-done | bytes 524320 | tf_op jit(solution)/shard_map/ppermute | solution.py:11
  43.4 1.3 broadcast_select_fusion
  44.8 6.3 collective-permute-start.2
  51.2 0.7 compare_and_fusion.1
  51.9 62.4 %collective-permute-done.2 = bf16[1024,256]{1,0:T(8,128)(2,1)S(1)} collective-permute-done((bf16[1024,256]{1,0:T(8,128)(2,1)S(1)}, bf16[1024,256]{1,0:T(8,128)(2,1)S(1)}, u32[]{:S(2)}, u32[]{:S(2)}) %collective-permute-start.2) | collective-permute-done | bytes 524320 | tf_op jit(solution)/shard_map/ppermute | solution.py:11
  114.3 1.9 collective-permute-start.3
  116.2 0.7 iota_compare_fusion.3
  116.9 0.7 slice_bitcast_fusion.2
  117.6 0.8 slice_bitcast_fusion.1
  118.4 34.3 %collective-permute-done.3 = bf16[1024,256]{1,0:T(8,128)(2,1)S(1)} collective-permute-done((bf16[1024,256]{1,0:T(8,128)(2,1)S(1)}, bf16[1024,256]{1,0:T(8,128)(2,1)S(1)}, u32[]{:S(2)}, u32[]{:S(2)}) %collective-permute-start.3) | collective-permute-done | bytes 524320 | tf_op jit(solution)/shard_map/ppermute | solution.py:11
  154.2 94.8 %while.20 = (s32[]{:T(128)}, bf16[1024,256]{1,0:T(8,128)(2,1)S(1)}, f32[8,128,256]{2,0,1:T(8,128)S(1)}, s32[1,8,2,8]{3,2,1,0:T(2,128)}, s32[1,8]{1,0:T(1,128)S(1...) while((s32[]{:T(128)}, bf16[1024,256]{1,0:T(8,128)(2,1)S(1)}, ...), condition=%wide.region_1.3_spmd.clone.clone, body=%wide.region_0.2_spmd.clone.clone.sunk | while | flops 72221880 | bytes 8067647 | solution.py:61
  154.2 2.3 collective-permute-start
  156.5 0.6 constant_dynamic-slice_fusion.5
  157.1 0.7 constant_dynamic-slice_fusion.4
  157.9 0.7 iota_compare_fusion.5
  158.6 0.9 dynamic-slice_bitcast_fusion.2
  159.4 3.8 collective-permute-done
  164.7 5.9 collective-permute-start
  170.6 0.6 constant_dynamic-slice_fusion.5
  171.2 0.7 constant_dynamic-slice_fusion.4
  172.0 0.7 iota_compare_fusion.5
  172.6 0.9 dynamic-slice_bitcast_fusion.2
  173.5 3.8 collective-permute-done
  178.7 5.9 collective-permute-start
  184.7 0.6 constant_dynamic-slice_fusion.5
  185.2 0.7 constant_dynamic-slice_fusion.4
  186.0 0.7 iota_compare_fusion.5
  186.7 0.9 dynamic-slice_bitcast_fusion.2
  187.6 3.8 collective-permute-done
  192.8 5.9 collective-permute-start
  198.7 0.6 constant_dynamic-slice_fusion.5
  199.3 0.7 constant_dynamic-slice_fusion.4
  200.1 0.7 iota_compare_fusion.5
  200.8 0.9 dynamic-slice_bitcast_fusion.2
  201.6 3.8 collective-permute-done
  206.8 5.9 collective-permute-start
  212.8 0.6 constant_dynamic-slice_fusion.5
  213.4 0.7 constant_dynamic-slice_fusion.4
  214.2 0.7 iota_compare_fusion.5
  214.8 0.9 dynamic-slice_bitcast_fusion.2
  215.7 3.8 collective-permute-done
  220.9 5.9 collective-permute-start
  226.8 0.6 constant_dynamic-slice_fusion.5
  227.4 0.7 constant_dynamic-slice_fusion.4
  228.2 0.7 iota_compare_fusion.5
  228.9 0.9 dynamic-slice_bitcast_fusion.2
  229.7 3.8 collective-permute-done
  235.0 5.9 collective-permute-start
  240.9 0.6 constant_dynamic-slice_fusion.5
  241.5 0.7 constant_dynamic-slice_fusion.4
  242.3 0.7 iota_compare_fusion.5
  243.0 0.9 dynamic-slice_bitcast_fusion.2
  243.8 3.8 collective-permute-done
  249.0 1.4 copy.14
  250.6 113.8 %all-gather.2.cloned.1.call-done = f32[8,1024,256]{2,1,0:T(8,128)} async-done(((f32[1,1024,256]{2,1,0:T(8,128)}), f32[8,1024,256]{2,1,0:T(8,128)}) %all-gather.2.cloned.1.call-update) | async-done | bytes 8388624 | tf_op jit(solution)/shard_map/all_gather | solution.py:65
  364.4 4.1 reduce_sum.9
  368.5 1.0 convolution_bitcast_fusion
  369.5 0.8 convolution_convert_fusion
  370.3 457.5 %all-reduce.2.cloned.1.call-done = f32[256,256]{0,1:T(8,128)} async-done(((f32[256,256]{0,1:T(8,128)}), f32[256,256]{0,1:T(8,128)}) %all-reduce.2.cloned.1.call-update) | async-done | bytes 262160 | tf_op jit(solution)/shard_map/psum | solution.py:75
  827.8 1.0 broadcast_multiply_fusion
  828.8 0.8 copy.15
  (82 shorter events, 12.4 us)
Async XLA Ops:
  7.2 362.3 %copy-start = (bf16[256,256]{1,0:T(8,128)(2,1)S(1)}, bf16[256,256]{1,0:T(8,128)(2,1)}, u32[]{:S(2)}) copy-start(bf16[256,256]{1,0:T(8,128)(2,1)} %param.13) | copy-start | bytes 393220
  7.2 147.0 %copy-start.2 = (s32[1,8]{1,0:T(1,128)S(1)}, s32[1,8]{1,0:T(1,128)}, u32[]{:S(2)}) copy-start(s32[1,8]{1,0:T(1,128)} %param.16) | copy-start | bytes 100
  7.2 357.2 %all-gather.2.cloned.1.call-start = ((), (), s32[]{:S(2)}) async-start(), calls=%async_computation | async-start | bytes 9437184 | tf_op jit(solution)/shard_map/all_gather | solution.py:65
  9.2 34.2 %collective-permute-start.1 = (bf16[1024,256]{1,0:T(8,128)(2,1)S(1)}, bf16[1024,256]{1,0:T(8,128)(2,1)S(1)}, u32[]{:S(2)}, u32[]{:S(2)}) collective-permute-start(bf16[1024,256]{1,0:T(8,128)(2,1)S(1)} %multiply_convert_fusion), channel_id=1, source_target_pairs={{64,0},{72,8},{80,16},{88,24},{96,32},{104,40},{112,48},{120,56},{... | collective-permute-start | bytes 1572872 | tf_op jit(solution)/shard_map/ppermute | solution.py:11
  44.8 69.5 %collective-permute-start.2 = (bf16[1024,256]{1,0:T(8,128)(2,1)S(1)}, bf16[1024,256]{1,0:T(8,128)(2,1)S(1)}, u32[]{:S(2)}, u32[]{:S(2)}) collective-permute-start(bf16[1024,256]{1,0:T(8,128)(2,1)S(1)} %broadcast_select_fusion), channel_id=1, source_target_pairs={{128,0},{136,8},{144,16},{152,24},{160,32},{168,40},{176,48},{184,... | collective-permute-start | bytes 1572872 | tf_op jit(solution)/shard_map/ppermute | solution.py:11
  114.3 38.5 %collective-permute-start.3 = (bf16[1024,256]{1,0:T(8,128)(2,1)S(1)}, bf16[1024,256]{1,0:T(8,128)(2,1)S(1)}, u32[]{:S(2)}, u32[]{:S(2)}) collective-permute-start(bf16[1024,256]{1,0:T(8,128)(2,1)S(1)} %broadcast_select_fusion.1), channel_id=1, source_target_pairs={{256,0},{264,8},{272,16},{280,24},{288,32},{296,40},{304,48},{312,... | collective-permute-start | bytes 1572872 | tf_op jit(solution)/shard_map/ppermute | solution.py:11
  154.2 9.0 %collective-permute-start = (bf16[1024,256]{1,0:T(8,128)(2,1)S(1)}, bf16[1024,256]{1,0:T(8,128)(2,1)S(1)}, u32[]{:S(2)}, u32[]{:S(2)}) collective-permute-start(bf16[1024,256]{1,0:T(8,128)(2,1)S(1)} %get-tuple-element.310), channel_id=1, source_target_pairs={{8,0},{16,8},{24,16},{32,24},{40,32},{48,40},{56,48},{64,56},{72,6... | collective-permute-start | bytes 1572872 | tf_op jit(solution)/shard_map/while/body/eval_jaxpr/ppermute | solution.py:11
  164.7 12.6 %collective-permute-start = (bf16[1024,256]{1,0:T(8,128)(2,1)S(1)}, bf16[1024,256]{1,0:T(8,128)(2,1)S(1)}, u32[]{:S(2)}, u32[]{:S(2)}) collective-permute-start(bf16[1024,256]{1,0:T(8,128)(2,1)S(1)} %get-tuple-element.310), channel_id=1, source_target_pairs={{8,0},{16,8},{24,16},{32,24},{40,32},{48,40},{56,48},{64,56},{72,6... | collective-permute-start | bytes 1572872 | tf_op jit(solution)/shard_map/while/body/eval_jaxpr/ppermute | solution.py:11
  178.7 12.6 %collective-permute-start = (bf16[1024,256]{1,0:T(8,128)(2,1)S(1)}, bf16[1024,256]{1,0:T(8,128)(2,1)S(1)}, u32[]{:S(2)}, u32[]{:S(2)}) collective-permute-start(bf16[1024,256]{1,0:T(8,128)(2,1)S(1)} %get-tuple-element.310), channel_id=1, source_target_pairs={{8,0},{16,8},{24,16},{32,24},{40,32},{48,40},{56,48},{64,56},{72,6... | collective-permute-start | bytes 1572872 | tf_op jit(solution)/shard_map/while/body/eval_jaxpr/ppermute | solution.py:11
  192.8 12.6 %collective-permute-start = (bf16[1024,256]{1,0:T(8,128)(2,1)S(1)}, bf16[1024,256]{1,0:T(8,128)(2,1)S(1)}, u32[]{:S(2)}, u32[]{:S(2)}) collective-permute-start(bf16[1024,256]{1,0:T(8,128)(2,1)S(1)} %get-tuple-element.310), channel_id=1, source_target_pairs={{8,0},{16,8},{24,16},{32,24},{40,32},{48,40},{56,48},{64,56},{72,6... | collective-permute-start | bytes 1572872 | tf_op jit(solution)/shard_map/while/body/eval_jaxpr/ppermute | solution.py:11
  206.8 12.6 %collective-permute-start = (bf16[1024,256]{1,0:T(8,128)(2,1)S(1)}, bf16[1024,256]{1,0:T(8,128)(2,1)S(1)}, u32[]{:S(2)}, u32[]{:S(2)}) collective-permute-start(bf16[1024,256]{1,0:T(8,128)(2,1)S(1)} %get-tuple-element.310), channel_id=1, source_target_pairs={{8,0},{16,8},{24,16},{32,24},{40,32},{48,40},{56,48},{64,56},{72,6... | collective-permute-start | bytes 1572872 | tf_op jit(solution)/shard_map/while/body/eval_jaxpr/ppermute | solution.py:11
  220.9 12.6 %collective-permute-start = (bf16[1024,256]{1,0:T(8,128)(2,1)S(1)}, bf16[1024,256]{1,0:T(8,128)(2,1)S(1)}, u32[]{:S(2)}, u32[]{:S(2)}) collective-permute-start(bf16[1024,256]{1,0:T(8,128)(2,1)S(1)} %get-tuple-element.310), channel_id=1, source_target_pairs={{8,0},{16,8},{24,16},{32,24},{40,32},{48,40},{56,48},{64,56},{72,6... | collective-permute-start | bytes 1572872 | tf_op jit(solution)/shard_map/while/body/eval_jaxpr/ppermute | solution.py:11
  235.0 12.6 %collective-permute-start = (bf16[1024,256]{1,0:T(8,128)(2,1)S(1)}, bf16[1024,256]{1,0:T(8,128)(2,1)S(1)}, u32[]{:S(2)}, u32[]{:S(2)}) collective-permute-start(bf16[1024,256]{1,0:T(8,128)(2,1)S(1)} %get-tuple-element.310), channel_id=1, source_target_pairs={{8,0},{16,8},{24,16},{32,24},{40,32},{48,40},{56,48},{64,56},{72,6... | collective-permute-start | bytes 1572872 | tf_op jit(solution)/shard_map/while/body/eval_jaxpr/ppermute | solution.py:11
  249.0 119.4 %copy-start.1 = (bf16[128,256]{1,0:T(8,128)(2,1)S(1)}, bf16[128,256]{1,0:T(8,128)(2,1)}, u32[]{:S(2)}) copy-start(bf16[128,256]{1,0:T(8,128)(2,1)} %param.11) | copy-start | bytes 196612
  250.5 577.4 %all-reduce.2.cloned.1.call-start = ((), (), s32[]{:S(2)}) async-start(), calls=%async_computation.1 | async-start | bytes 524288 | tf_op jit(solution)/shard_map/psum | solution.py:75
Sparse Core Ops, SparseCore 0:
  250.6 113.7 all-gather.1
  370.4 457.3 all-reduce.1
